TPU v7x, 1024 devices: a whole 4x4x32 slice. The times are simulated.
1024 devices in a mesh: row: 16 (over z_hi, y), col: 16 (over z_lo, core), depth: 4 (over x).
Axes of the slice: x: 4, y: 4, z: 32 (z_hi: 4, z_lo: 8; z = z_hi * 8 + z_lo), core: 2. Of those that a mesh axis runs over, the one named last changes fastest.
Arguments:
- gate_pre: bfloat16 [2048, 26624], P(('col', 'depth'), 'row'), may hold values from -6 to 6
- up_pre: bfloat16 [2048, 26624], P(('col', 'depth'), 'row'), may hold values from -6 to 6
- out_grad: bfloat16 [2048, 16384], P(('row', 'depth'), 'col'), may hold values from -2 to 2
- down_weight: bfloat16 [26624, 16384], P('row', 'col'), may hold values from -0.0390625 to 0.0390625
Outputs:
- weight_grad: bfloat16 [26624, 16384], P(('row', 'depth'), 'col')
- gate_grad: bfloat16 [2048, 26624], P(('col', 'depth'), 'row')
- up_grad: bfloat16 [2048, 26624], P(('col', 'depth'), 'row')
All inputs are finite; a program needn't handle non-finite values.
Results may differ from a plain program's by a relative error of at most 0.009.
Values may be sent and summed in bfloat16 or wider, within the bound.
A program may use at most 64 MiB of HBM per device.

v0:
```python
import jax
import jax.numpy as jnp
from jax import lax
from jax.sharding import Mesh
from jax.sharding import PartitionSpec as P

COL = ("col_0", "col_1")
COL_DEPTH = ("col_0", "col_1", "depth")


def sent_together(arrays, axis, dim, along):
    widths = [a.shape[along] for a in arrays]
    both = jnp.concatenate(arrays, axis=along)
    out = lax.all_gather(both, axis, axis=dim, tiled=True)
    return tuple(jnp.split(out, [sum(widths[:k]) for k in range(1, len(widths))], axis=along))


def sum_in_order(parts, axes, sequence):
    lengths = [lax.axis_size(a) for a in axes]
    parts = parts.reshape(*lengths, *parts.shape[1:])
    parts = parts.transpose(*sequence, *range(len(axes), parts.ndim))
    parts = parts.reshape(-1, *parts.shape[len(axes) :])
    for k in sequence:
        parts = lax.psum_scatter(parts, axes[k], scatter_dimension=0, tiled=True)
    return parts[0]


def split_up(array, dim, devices):
    before, after = (array.shape[:dim], array.shape[dim + 1 :])
    return jnp.moveaxis(array.reshape(*before, devices, -1, *after), dim, 0)


def summed_rows(array, axes, sequence, dim):
    devices = lax.axis_size(axes)
    return sum_in_order(split_up(array, dim, devices), axes, sequence)


def sent_and_summed(array, axis, dim):
    parts = split_up(array, dim, lax.axis_size(axis))
    arrived = lax.all_to_all(parts, axis, split_axis=0, concat_axis=0, tiled=True)
    return arrived.astype(jnp.float32).sum(axis=0)


def on_device(gate_pre, up_pre, out_grad, down_weight):
    gate_vals = gate_pre.astype(jnp.float32)
    up_vals = up_pre.astype(jnp.float32)
    sigma_gate = jax.nn.sigmoid(gate_vals)
    act = gate_vals * sigma_gate
    gate_all, up_all = sent_together((gate_pre, up_pre), COL, 0, 1)
    gate_wide = gate_all.astype(jnp.float32)
    hidden_all = (gate_wide * jax.nn.sigmoid(gate_wide) * up_all.astype(jnp.float32)).astype(
        jnp.bfloat16
    )
    grads_all = lax.all_gather(out_grad, "row", axis=0, tiled=True)
    weight_terms = lax.dot_general(
        hidden_all, grads_all, (((0,), (0,)), ((), ())), preferred_element_type=jnp.float32
    )
    hidden_terms = lax.dot_general(
        grads_all, down_weight, (((1,), (1,)), ((), ())), preferred_element_type=jnp.float32
    )
    hidden_grad = summed_rows(hidden_terms, COL, (1, 0), 0)
    up_grad = (hidden_grad * act).astype(jnp.bfloat16)
    gate_grad = (
        hidden_grad * up_vals * sigma_gate * (1.0 + gate_vals * (1.0 - sigma_gate))
    ).astype(jnp.bfloat16)
    layer_partial = weight_terms.astype(jnp.bfloat16)
    weight_grad = sent_and_summed(layer_partial, "depth", 0).astype(jnp.bfloat16)
    return (weight_grad, gate_grad, up_grad)


def solution(mesh):
    torus = Mesh(
        mesh.devices.reshape(mesh.shape["row"], 8, 2, mesh.shape["depth"]),
        ("row", "col_0", "col_1", "depth"),
    )
    in_specs = (P(COL_DEPTH, "row"), P(COL_DEPTH, "row"), P(("row", "depth"), COL), P("row", COL))
    out_specs = (P(("row", "depth"), COL), P(COL_DEPTH, "row"), P(COL_DEPTH, "row"))
    return jax.shard_map(
        on_device, mesh=torus, in_specs=in_specs, out_specs=out_specs, check_vma=False
    )
```

profile of v0, /device:TPU:8, one launch (start us, length us, event | category | flops | bytes accessed | tf_op | source)
XLA Modules:
  0.0 333.4 jit_solution(911235975987557496)
XLA Ops:
  8.0 0.0 copy-start
  8.0 0.0 all-gather.5.cloned.1.call-start
  8.1 0.7 all-gather.5.cloned.1.call-update
  8.7 0.0 reduce-scatter.3.cloned.1.call-start
  8.8 140.9 %all-gather.5.cloned.1.call-done = bf16[512,1024]{1,0:T(8,128)(2,1)} async-done(((bf16[32,1024]{1,0:T(8,128)(2,1)}), bf16[512,1024]{1,0:T(8,128)(2,1)}) %all-gather.5.cloned.1.call-update) | async-done | bytes 1048592 | tf_op jit(solution)/shard_map/all_gather | solution.py:54
  149.7 0.0 copy-done
  149.7 3.3 fusion.19
  153.0 2.0 copy.7
  155.0 0.0 copy-start.1
  155.0 0.0 reduce-scatter.3.cloned.1.call-update
  155.1 0.0 all-gather.3.cloned.1.call-start
  155.1 0.8 copy-done.1
  155.9 1.6 pad_maximum_fusion
  157.5 0.0 all-gather.3.cloned.1.call-update
  157.6 0.0 reduce-scatter.5.cloned.1.call-start
  157.6 19.2 %reduce-scatter.3.cloned.1.call-done = f32[8,32,1664]{2,1,0:T(8,128)} async-done(((f32[16,32,1664]{2,1,0:T(8,128)}), f32[8,32,1664]{2,1,0:T(8,128)}) %reduce-scatter.3.cloned.1.call-update) | async-done | bytes 1703952 | tf_op jit(solution)/shard_map/reduce_scatter | solution.py:24
  176.8 0.0 reduce-scatter.5.cloned.1.call-update
  176.8 95.1 %all-gather.3.cloned.1.call-done = bf16[512,3328]{1,0:T(8,128)(2,1)} async-done(((bf16[32,3328]{1,0:T(8,128)(2,1)}), bf16[512,3328]{1,0:T(8,128)(2,1)}) %all-gather.3.cloned.1.call-update) | async-done | bytes 3407888 | tf_op jit(solution)/shard_map/all_gather | solution.py:14
  271.9 4.5 %convolution_convert_fusion = bf16[1664,1024]{1,0:T(8,128)(2,1)S(1)} fusion(bf16[512,1024]{1,0:T(8,128)(2,1)} %all-gather.5.cloned.1.call-done, bf16[512,3328]{1,0:T(8,128)(2,1)} %all-gather.3.cloned.1.call-done), kind=kOutput, calls=%fused_computation.2 | convolution fusion | flops 1753350144 | bytes 7864320 | tf_op jit(solution)/shard_map/dot_general | solution.py:55
  276.5 44.2 %all_to_all.5 = bf16[4,416,1024]{2,1,0:T(8,128)(2,1)} all-to-all(bf16[4,416,1024]{2,1,0:T(8,128)(2,1)S(1)} %bitcast.16), channel_id=1, replica_groups=mesh['row'=16,'col_0'=8,'col_1'=2,'depth'=4] {'depth'}, dimensions={0} | all-to-all | bytes 6815744 | tf_op jit(solution)/shard_map/all_to_all | solution.py:40
  320.7 3.8 %reduce_sum.12 = bf16[416,1024]{1,0:T(8,128)(2,1)} reduce(bf16[4,416,1024]{2,1,0:T(8,128)(2,1)} %all_to_all.5, bf16[]{:T(256)} %constant.1.clone.1), dimensions={0}, to_apply=%region_0.0 | reduce | flops 1277952 | bytes 4259842 | tf_op jit(solution)/shard_map/reduce_sum | solution.py:41
  324.5 0.0 reduce-scatter.5.cloned.1.call-done
  324.5 1.8 fusion.16
Async XLA Ops:
  8.0 141.7 %copy-start = (bf16[1664,1024]{1,0:T(8,128)(2,1)S(1)}, bf16[1664,1024]{1,0:T(8,128)(2,1)}, u32[]{:S(2)}) copy-start(bf16[1664,1024]{1,0:T(8,128)(2,1)} %param.7) | copy-start | bytes 10223620
  8.0 141.7 %all-gather.5.cloned.1.call-start = ((), (), s32[]{:S(2)}) async-start(), calls=%async_computation.4 | async-start | bytes 1114112 | tf_op jit(solution)/shard_map/all_gather | solution.py:54
  8.7 168.0 %reduce-scatter.3.cloned.1.call-start = ((), (), s32[]{:S(2)}) async-start(), calls=%async_computation.5 | async-start | bytes 5111808 | tf_op jit(solution)/shard_map/reduce_scatter | solution.py:24
  155.0 0.9 copy-start.1
  155.1 116.9 %all-gather.3.cloned.1.call-start = ((), (), s32[]{:S(2)}) async-start(), calls=%async_computation.3 | async-start | bytes 3620864 | tf_op jit(solution)/shard_map/all_gather | solution.py:14
  157.6 166.9 %reduce-scatter.5.cloned.1.call-start = ((), (), s32[]{:S(2)}) async-start(), calls=%async_computation.6 | async-start | bytes 1916928 | tf_op jit(solution)/shard_map/reduce_scatter | solution.py:24
Sparse Core Ops, SparseCore 0:
  13.0 136.6 all-gather.4
  155.2 21.5 reduce-scatter.2
  180.6 85.0 reduce-scatter.4
Sparse Core Ops, SparseCore 1:
  158.8 113.1 all-gather.2
where the time goes:
time: 334 us; the launch traced here: 333 us
  waiting for transfers between devices  256 us (77%)
  blocking collectives  44.2 us (13%)
  between operations  15.2 us (5%)
  matrix products  7.85 us (2%)
  other arithmetic  7.18 us (2%)
    all_gather x1, waiting for transfers between devices, on_device(): grads_all = lax.all_gather(out_grad, 'row', axis=0, tiled=True)  141 us
    all_gather x1, waiting for transfers between devices, sent_together(): out = lax.all_gather(both, axis, axis=dim, tiled=True)  95.1 us
    all_to_all x1, blocking collectives, sent_and_summed(): lax.all_to_all(parts, axis, split_axis=0, concat_axis=0, tiled=True)  44.2 us
    reduce_scatter x2, waiting for transfers between devices, sum_in_order(): parts = lax.psum_scatter(parts, axes[k], scatter_dimension=0, tiled=True)  19.2 us
  transfers between devices with their start and end apart: 4, of which 3 were waited for; matrix products, arithmetic and copies ran while one was open for 3% of the time, Pallas kernels for 0%

commit v1 on v0

v1 whole, which is shorter than its diff:
```python
import functools

import jax
import jax.numpy as jnp
from jax import lax
from jax.experimental import pallas as pl
from jax.experimental.pallas import tpu as pltpu
from jax.sharding import Mesh
from jax.sharding import PartitionSpec as P

MESH = pl.DeviceIdType.MESH
COL = ("zl", "core")
ROW = ("zh", "y")
F32 = jnp.float32
BF16 = jnp.bfloat16
NT = (((1,), (1,)), ((), ()))


def kernel(
    gate_ref, up_ref, og_ref, w_ref,
    dw_ref, gg_ref, ug_ref,
    G, W, gv, uv, act, fac, HS, HX, HT, PF, PB, PR, RB, SB, HG, ACC,
    lsem, zs, zr, ys, yr, xs, xr, hs, hr, brs, brr, bls, blr, bps, bpr, ps, pr, cs, cr,
):
    zo, y, k, c, x = (lax.axis_index(a) for a in ("zh", "y", "zl", "core", "x"))
    zp, zm = lax.rem(zo + 1, 4), lax.rem(zo + 3, 4)
    yp, ym = lax.rem(y + 1, 4), lax.rem(y + 3, 4)
    xp, xm = lax.rem(x + 1, 4), lax.rem(x + 3, 4)
    sends = []

    def copy(src, dst, ss, rs, dev):
        return pltpu.make_async_remote_copy(
            src_ref=src, dst_ref=dst, send_sem=ss, recv_sem=rs, device_id=dev, device_id_type=MESH
        )

    def send(*args):
        cp = copy(*args)
        cp.start()
        sends.append(cp)

    loads = [
        pltpu.make_async_copy(og_ref, G.at[zo, y, x], lsem.at[0]),
        pltpu.make_async_copy(gate_ref, gv, lsem.at[1]),
        pltpu.make_async_copy(up_ref, uv, lsem.at[2]),
        pltpu.make_async_copy(w_ref, W, lsem.at[3]),
    ]
    for cp in loads:
        cp.start()
    barrier = pltpu.get_barrier_semaphore()
    peers = [{"zh": zp}, {"zh": zm}, {"y": yp}, {"y": ym}, {"x": xp}, {"x": xm},
             {"x": lax.rem(x + 2, 4)}, {"core": 1 - c}, {"zl": lax.rem(k + 1, 8)}, {"zl": lax.rem(k + 7, 8)}]
    for dev in peers:
        pl.semaphore_signal(barrier, inc=1, device_id=dev, device_id_type=MESH)

    loads[1].wait()
    loads[2].wait()
    g = gv[...].astype(F32)
    u = uv[...].astype(F32)
    sig = jax.nn.sigmoid(g)
    a = g * sig
    act[...] = a
    fac[...] = u * sig * (1.0 + g * (1.0 - sig))
    h = a * u
    for s in range(4):
        rolled = h if s == 0 else pltpu.roll(h, 1664 - 416 * s, 1)
        HS[s] = rolled[:, :512].astype(BF16)
    loads[0].wait()

    pl.semaphore_wait(barrier, len(peers))

    def half(i):
        return pl.ds(16 * i, 16)

    def z_first():
        own = G.at[zo, y, x]
        for i, (hp, hm) in enumerate(((0, 1), (1, 0))):
            send(own.at[half(hp)], own.at[half(hp)], zs.at[0, i], zr.at[0, i], {"zh": zp})
            send(own.at[half(hm)], own.at[half(hm)], zs.at[1, i], zr.at[1, i], {"zh": zm})

    def z_wait(d, i):
        zh = (zm, zp)[d] if i < 2 else lax.rem(zo + 2, 4)
        hh = d if i != 1 else 1 - d
        dst = G.at[zh, y, x].at[half(hh)]
        copy(dst, dst, zs.at[d, i], zr.at[d, i], {"zh": zp}).wait_recv()

    def z_relay():
        z_wait(0, 0)
        r = G.at[zm, y, x].at[half(0)]
        send(r, r, zs.at[0, 2], zr.at[0, 2], {"zh": zp})
        z_wait(1, 0)
        r = G.at[zp, y, x].at[half(1)]
        send(r, r, zs.at[1, 2], zr.at[1, 2], {"zh": zm})
        z_wait(0, 1)
        z_wait(1, 1)

    def y_first(q):
        b = G.at[lax.rem(zo + q, 4), y, x]
        send(b, b, ys.at[q, 0], yr.at[q, 0], {"y": yp})
        send(b, b, ys.at[q, 1], yr.at[q, 1], {"y": ym})

    def y_relay(q):
        zh = lax.rem(zo + q, 4)
        b = G.at[zh, ym, x]
        copy(b, b, ys.at[q, 0], yr.at[q, 0], {"y": yp}).wait_recv()
        b = b.at[half(0)]
        send(b, b, ys.at[q, 2], yr.at[q, 2], {"y": yp})
        b = G.at[zh, yp, x]
        copy(b, b, ys.at[q, 1], yr.at[q, 1], {"y": yp}).wait_recv()
        b = b.at[half(1)]
        send(b, b, ys.at[q, 3], yr.at[q, 3], {"y": ym})

    def y_last(q):
        b = G.at[lax.rem(zo + q, 4), lax.rem(y + 2, 4), x]
        for i in range(2):
            d = b.at[half(i)]
            copy(d, d, ys.at[q, 2 + i], yr.at[q, 2 + i], {"y": yp}).wait_recv()

    def x_first(q):
        b = G.at[lax.rem(zo + q, 4), :, x]
        send(b, b, xs.at[q, 0], xr.at[q, 0], {"x": xp})
        send(b, b, xs.at[q, 1], xr.at[q, 1], {"x": xm})

    def x_relay(q):
        zh = lax.rem(zo + q, 4)
        b = G.at[zh, :, xm]
        copy(b, b, xs.at[q, 0], xr.at[q, 0], {"x": xp}).wait_recv()
        b = G.at[zh, pl.ds(0, 2), xm]
        send(b, b, xs.at[q, 2], xr.at[q, 2], {"x": xp})
        b = G.at[zh, :, xp]
        copy(b, b, xs.at[q, 1], xr.at[q, 1], {"x": xp}).wait_recv()
        b = G.at[zh, pl.ds(2, 2), xp]
        send(b, b, xs.at[q, 3], xr.at[q, 3], {"x": xm})

    def x_last(q):
        zh = lax.rem(zo + q, 4)
        for i in range(2):
            d = G.at[zh, pl.ds(2 * i, 2), lax.rem(x + 2, 4)]
            copy(d, d, xs.at[q, 2 + i], xr.at[q, 2 + i], {"x": xp}).wait_recv()

    def h_first():
        for o in range(1, 4):
            to = lax.rem(x + o, 4)
            send(HS.at[to], HX.at[x], hs.at[o - 1], hr.at[o - 1], {"x": to})
        HX[x] = HS[x]

    def h_last():
        for o in range(1, 4):
            d = HX.at[lax.rem(x + 4 - o, 4)]
            copy(d, d, hs.at[o - 1], hr.at[o - 1], {"x": xp}).wait_recv()
        t = HX[...].astype(F32).reshape(128, 512).T
        HT[2 * k + c] = t[:416].astype(BF16)

    def ht(o, i):
        return HT.at[2 * o + c, pl.ds(208 * i, 208)]

    def right(o, i, idx):
        b = ht(o, i)
        return copy(b, b, brs.at[idx], brr.at[idx], {"zl": k + 1})

    def left(o, i, idx):
        b = ht(o, i)
        return copy(b, b, bls.at[idx], blr.at[idx], {"zl": k - 1})

    def across(o):
        return copy(HT.at[2 * o + c], HT.at[2 * o + c], bps.at[o], bpr.at[o], {"core": 1 - c})

    def b_first():
        for i in range(2):
            @pl.when(k < 7)
            def _():
                right(k, i, i).start()

            @pl.when(k > 0)
            def _():
                left(k, i, i).start()
        across(k).start()

    def b_steps(lo, hi):
        def step(s, carry):
            for i in range(2):
                @pl.when(k - 1 - s >= 0)
                def _():
                    o = k - 1 - s
                    right(o, i, 2 * s + i).wait_recv()

                    @pl.when(k < 7)
                    def _():
                        right(o, i, 2 * s + 2 + i).start()

                @pl.when(k + 1 + s <= 7)
                def _():
                    o = k + 1 + s
                    left(o, i, 2 * s + i).wait_recv()

                    @pl.when(k > 0)
                    def _():
                        left(o, i, 2 * s + 2 + i).start()

            @pl.when(k - 1 - s >= 0)
            def _():
                across(k - 1 - s).start()

            @pl.when(k + 1 + s <= 7)
            def _():
                across(k + 1 + s).start()

            return carry

        lax.fori_loop(lo, hi, step, 0)

    def b_last():
        def step(o, carry):
            d = HT.at[2 * o + 1 - c]
            copy(d, d, bps.at[o], bpr.at[o], {"core": 1 - c}).wait_recv()
            return carry

        lax.fori_loop(0, 8, step, 0)

    def terms(q):
        zh = lax.rem(zo + q, 4)
        rows = G[zh, :, x].reshape(128, 1024)

        def part(n0, nn):
            res = lax.dot_general(rows, W[pl.ds(n0, nn), :], NT, preferred_element_type=F32)
            res = res.reshape(2, 2, 32, nn)
            PF[pl.ds(2 * zh, 2), :, :, pl.ds(n0, nn)] = res
            PB[pl.ds(2 * zh, 2), :, :, pl.ds(n0, nn)] = res.astype(BF16)

        def step(i, carry):
            part(pl.multiple_of(i * 256, 256), 256)
            return carry

        lax.fori_loop(0, 6, step, 0)
        part(1536, 128)
        send(PB.at[pl.ds(2 * zh, 2), 1 - c], PR.at[pl.ds(2 * zh, 2)], ps.at[q], pr.at[q], {"core": 1 - c})

    def terms_last(q):
        zh = lax.rem(zo + q, 4)
        d = PR.at[pl.ds(2 * zh, 2)]
        copy(d, d, ps.at[q], pr.at[q], {"core": 1 - c}).wait_recv()

    def c_copy(way, d, i, dev):
        return copy(SB.at[d, half(i)], RB.at[way, d, half(i)], cs.at[d, i], cr.at[way, d, i], dev)

    def c_steps(lo, hi):
        def one(way, pos, d, i, to):
            mine = PF[d, c, half(i)] + PR[d, half(i)].astype(F32)

            @pl.when(pos == 0)
            def _():
                SB[d, half(i)] = mine.astype(BF16)

            @pl.when(pos > 0)
            def _():
                c_copy(way, d, i, {"zl": to}).wait_recv()
                SB[d, half(i)] = (mine + RB[way, d, half(i)].astype(F32)).astype(BF16)

            c_copy(way, d, i, {"zl": to}).start()

        def step(t, carry):
            for i in range(2):
                q = t - k - i
                j = q // 2

                @pl.when((q >= 0) & (lax.rem(q + 16, 2) == 0) & (7 - j > k))
                def _():
                    one(0, k, 7 - j, i, k + 1)

                r = t - (7 - k) - i
                m = r // 2

                @pl.when((r >= 0) & (lax.rem(r + 16, 2) == 0) & (m < k))
                def _():
                    one(1, 7 - k, m, i, k - 1)

            return carry

        lax.fori_loop(lo, hi, step, 0)

    def c_last():
        HG[...] = PF[k, c] + PR[k].astype(F32)

        @pl.when(k > 0)
        def _():
            for i in range(2):
                c_copy(0, k, i, {"zl": k - 1}).wait_recv()
            HG[...] += RB[0, k].astype(F32)

        @pl.when(k < 7)
        def _():
            for i in range(2):
                c_copy(1, k, i, {"zl": k + 1}).wait_recv()
            HG[...] += RB[1, k].astype(F32)

        hg = HG[...]
        ug_ref[...] = (hg * act[...]).astype(BF16)
        gg_ref[...] = (hg * fac[...]).astype(BF16)

    def dw(q, first=False):
        zh = lax.rem(zo + q, 4)
        lhs = jnp.concatenate([HT[4 * zh + i] for i in range(4)], axis=1)

        def step(n, carry):
            cols = pl.ds(pl.multiple_of(n * 256, 256), 256)
            rhs = G[zh, :, :, :, cols].reshape(512, 256)
            res = jnp.dot(lhs, rhs, preferred_element_type=F32)
            ACC[:, cols] = res if first else ACC[:, cols] + res
            return carry

        lax.fori_loop(0, 4, step, 0)

    z_first()
    y_first(0)
    h_first()
    h_last()
    b_first()
    y_relay(0)
    y_last(0)
    x_first(0)
    loads[3].wait()
    terms(0)
    b_steps(0, 2)
    z_relay()
    y_first(1)
    y_first(3)
    b_steps(2, 3)
    y_relay(1)
    y_relay(3)
    x_relay(0)
    y_last(1)
    y_last(3)
    x_first(1)
    x_first(3)
    terms(1)
    terms(3)
    b_steps(3, 4)
    z_wait(0, 2)
    z_wait(1, 2)
    y_first(2)
    b_steps(4, 5)
    y_relay(2)
    y_last(2)
    x_first(2)
    terms(2)
    b_steps(5, 7)
    for q in range(4):
        terms_last(q)
    x_relay(1)
    x_relay(3)
    c_steps(0, 4)
    b_last()
    x_last(0)
    dw(0, True)
    c_steps(4, 7)
    x_relay(2)
    x_last(1)
    dw(1)
    c_steps(7, 10)
    x_last(3)
    dw(3)
    c_steps(10, 14)
    x_last(2)
    dw(2)
    dw_ref[...] = ACC[...].astype(BF16)
    c_last()

    for cp in sends:
        cp.wait_send()

    def drain_b(s, carry):
        for i in range(2):
            @pl.when((k - s >= 0) & (k < 7))
            def _():
                right(k - s, i, 2 * s + i).wait_send()

            @pl.when((k + s <= 7) & (k > 0))
            def _():
                left(k + s, i, 2 * s + i).wait_send()

        across(s).wait_send()
        return carry

    lax.fori_loop(0, 8, drain_b, 0)

    def drain_c(d, carry):
        @pl.when(d != k)
        def _():
            for i in range(2):
                c_copy(0, d, i, {"core": 1 - c}).wait_send()

        return carry

    lax.fori_loop(0, 8, drain_c, 0)


def on_device(gate_pre, up_pre, out_grad, down_weight):
    dma = pltpu.SemaphoreType.DMA
    any_spec = pl.BlockSpec(memory_space=pl.ANY)
    vmem = pl.BlockSpec(memory_space=pltpu.VMEM)
    act_shape = (32, 1664)
    return pl.pallas_call(
        kernel,
        out_shape=(
            jax.ShapeDtypeStruct((416, 1024), BF16),
            jax.ShapeDtypeStruct(act_shape, BF16),
            jax.ShapeDtypeStruct(act_shape, BF16),
        ),
        in_specs=[any_spec] * 4,
        out_specs=(vmem,) * 3,
        scratch_shapes=[
            pltpu.VMEM((4, 4, 4, 32, 1024), BF16),
            pltpu.VMEM((1664, 1024), BF16),
            pltpu.VMEM(act_shape, BF16),
            pltpu.VMEM(act_shape, BF16),
            pltpu.VMEM(act_shape, F32),
            pltpu.VMEM(act_shape, F32),
            pltpu.VMEM((4, 32, 512), BF16),
            pltpu.VMEM((4, 32, 512), BF16),
            pltpu.VMEM((16, 416, 128), BF16),
            pltpu.VMEM((8, 2, 32, 1664), F32),
            pltpu.VMEM((8, 2, 32, 1664), BF16),
            pltpu.VMEM((8, 32, 1664), BF16),
            pltpu.VMEM((2, 8, 32, 1664), BF16),
            pltpu.VMEM((8, 32, 1664), BF16),
            pltpu.VMEM(act_shape, F32),
            pltpu.VMEM((416, 1024), F32),
            dma((4,)),
            dma((2, 3)), dma((2, 3)),
            dma((4, 4)), dma((4, 4)),
            dma((4, 4)), dma((4, 4)),
            dma((3,)), dma((3,)),
            dma((16,)), dma((16,)),
            dma((16,)), dma((16,)),
            dma((8,)), dma((8,)),
            dma((4,)), dma((4,)),
            dma((8, 2)), dma((2, 8, 2)),
        ],
        compiler_params=pltpu.CompilerParams(
            collective_id=0, has_side_effects=True, vmem_limit_bytes=48 * 1024 * 1024
        ),
    )(gate_pre, up_pre, out_grad, down_weight)


def solution(mesh):
    torus = Mesh(mesh.devices.reshape(4, 4, 8, 2, 4), ("zh", "y", "zl", "core", "x"))
    in_specs = (
        P(("zl", "core", "x"), ROW),
        P(("zl", "core", "x"), ROW),
        P(("zh", "y", "x"), COL),
        P(ROW, COL),
    )
    out_specs = (P(("zh", "y", "x"), COL), P(("zl", "core", "x"), ROW), P(("zl", "core", "x"), ROW))
    return jax.shard_map(
        on_device, mesh=torus, in_specs=in_specs, out_specs=out_specs, check_vma=False
    )
```

time: 334 us -> 113 us (0.34)
  the two profiles are of different devices: /device:TPU:8 before, /device:TPU:66 now
where the time goes in v1:
time: 113 us
  Pallas kernels  105 us (93%)
  local copies, waits for them, and re-layouts  6.78 us (6%)
    pallas_call x1, Pallas kernels, on_device(): pl.pallas_call(kernel, out_shape=(jax.ShapeDtypeStruct((416, 1024), BF16)...  105 us
    unnamed x11, local copies, waits for them, and re-layouts  6.78 us

profile of v1, /device:TPU:66, one launch (start us, length us, event | category | flops | bytes accessed | tf_op | source)
XLA Modules:
  0.0 112.8 jit_solution(2369043816175632275)
XLA Ops:
  0.6 0.0 copy-start
  0.6 2.0 %copy-done = bf16[1664,1024]{1,0:T(8,128)(2,1)S(1)} copy-done((bf16[1664,1024]{1,0:T(8,128)(2,1)S(1)}, bf16[1664,1024]{1,0:T(8,128)(2,1)}, u32[]{:S(2)}) %copy-start) | copy-done | bytes 3407896
  2.6 0.0 copy-start.1
  2.6 0.9 copy-done.1
  3.5 0.0 copy-start.2
  3.5 0.9 copy-done.2
  4.4 0.0 copy-start.3
  4.4 0.8 copy-done.3
  5.2 105.4 %shard_map.67 = (bf16[416,1024]{1,0:T(8,128)(2,1)S(1)}, bf16[32,1664]{1,0:T(8,128)(2,1)S(1)}, bf16[32,1664]{1,0:T(8,128)(2,1)S(1)}) custom-call(bf16[32,1664]{1,0:T(8,128)(2,1)S(1)} %copy-done.1, bf16[32,1664]{1,0:T(8,128)(2,1)S(1)} %copy-done.2, bf16[32,1024]{1,0:T(8,128)(2,1)S(1)} %copy-done.3, bf16[1664,1024]{1,0:T(8,128)(2,1)S(1)} %copy-done), custom_call_target="tpu_custom_call" | custom-call | tf_op jit(solution)/shard_map/pallas_call | solution.py:401
  110.6 0.9 copy.10
  111.5 0.6 copy.11
  112.2 0.6 copy.12
Async XLA Ops:
  0.6 2.0 %copy-start = (bf16[1664,1024]{1,0:T(8,128)(2,1)S(1)}, bf16[1664,1024]{1,0:T(8,128)(2,1)}, u32[]{:S(2)}) copy-start(bf16[1664,1024]{1,0:T(8,128)(2,1)} %w_ref.1) | copy-start | bytes 10223620
  2.6 0.9 copy-start.1
  3.5 0.9 copy-start.2
  4.4 0.8 copy-start.3

commit v2 on v1

--- a/solution.py
+++ b/solution.py
@@ -14,6 +14,7 @@
 F32 = jnp.float32
 BF16 = jnp.bfloat16
 NT = (((1,), (1,)), ((), ()))
+NB = 2
 
 
 def kernel(
@@ -38,6 +39,11 @@
         cp.start()
         sends.append(cp)
 
+    barrier = pltpu.get_barrier_semaphore()
+    peers = [{"zh": zp}, {"zh": zm}, {"y": yp}, {"y": ym}, {"x": xp}, {"x": xm},
+             {"x": lax.rem(x + 2, 4)}, {"core": 1 - c}, {"zl": lax.rem(k + 1, 8)}, {"zl": lax.rem(k + 7, 8)}]
+    for dev in peers:
+        pl.semaphore_signal(barrier, inc=1, device_id=dev, device_id_type=MESH)
     loads = [
         pltpu.make_async_copy(og_ref, G.at[zo, y, x], lsem.at[0]),
         pltpu.make_async_copy(gate_ref, gv, lsem.at[1]),
@@ -46,26 +52,7 @@
     ]
     for cp in loads:
         cp.start()
-    barrier = pltpu.get_barrier_semaphore()
-    peers = [{"zh": zp}, {"zh": zm}, {"y": yp}, {"y": ym}, {"x": xp}, {"x": xm},
-             {"x": lax.rem(x + 2, 4)}, {"core": 1 - c}, {"zl": lax.rem(k + 1, 8)}, {"zl": lax.rem(k + 7, 8)}]
-    for dev in peers:
-        pl.semaphore_signal(barrier, inc=1, device_id=dev, device_id_type=MESH)
-
-    loads[1].wait()
-    loads[2].wait()
-    g = gv[...].astype(F32)
-    u = uv[...].astype(F32)
-    sig = jax.nn.sigmoid(g)
-    a = g * sig
-    act[...] = a
-    fac[...] = u * sig * (1.0 + g * (1.0 - sig))
-    h = a * u
-    for s in range(4):
-        rolled = h if s == 0 else pltpu.roll(h, 1664 - 416 * s, 1)
-        HS[s] = rolled[:, :512].astype(BF16)
     loads[0].wait()
-
     pl.semaphore_wait(barrier, len(peers))
 
     def half(i):
@@ -90,6 +77,7 @@
         z_wait(1, 0)
         r = G.at[zp, y, x].at[half(1)]
         send(r, r, zs.at[1, 2], zr.at[1, 2], {"zh": zm})
+    def z_second():
         z_wait(0, 1)
         z_wait(1, 1)
 
@@ -137,6 +125,20 @@
             d = G.at[zh, pl.ds(2 * i, 2), lax.rem(x + 2, 4)]
             copy(d, d, xs.at[q, 2 + i], xr.at[q, 2 + i], {"x": xp}).wait_recv()
 
+    def hidden():
+        loads[1].wait()
+        loads[2].wait()
+        g = gv[...].astype(F32)
+        u = uv[...].astype(F32)
+        sig = jax.nn.sigmoid(g)
+        a = g * sig
+        act[...] = a
+        fac[...] = u * sig * (1.0 + g * (1.0 - sig))
+        h = a * u
+        for s in range(4):
+            rolled = h if s == 0 else pltpu.roll(h, 1664 - 416 * s, 1)
+            HS[s] = rolled[:, :512].astype(BF16)
+
     def h_first():
         for o in range(1, 4):
             to = lax.rem(x + o, 4)
@@ -151,7 +153,7 @@
         HT[2 * k + c] = t[:416].astype(BF16)
 
     def ht(o, i):
-        return HT.at[2 * o + c, pl.ds(208 * i, 208)]
+        return HT.at[2 * o + c, pl.ds(416 // NB * i, 416 // NB)]
 
     def right(o, i, idx):
         b = ht(o, i)
@@ -165,7 +167,7 @@
         return copy(HT.at[2 * o + c], HT.at[2 * o + c], bps.at[o], bpr.at[o], {"core": 1 - c})
 
     def b_first():
-        for i in range(2):
+        for i in range(NB):
             @pl.when(k < 7)
             def _():
                 right(k, i, i).start()
@@ -177,24 +179,24 @@
 
     def b_steps(lo, hi):
         def step(s, carry):
-            for i in range(2):
+            for i in range(NB):
                 @pl.when(k - 1 - s >= 0)
                 def _():
                     o = k - 1 - s
-                    right(o, i, 2 * s + i).wait_recv()
+                    right(o, i, NB * s + i).wait_recv()
 
                     @pl.when(k < 7)
                     def _():
-                        right(o, i, 2 * s + 2 + i).start()
+                        right(o, i, NB * s + NB + i).start()
 
                 @pl.when(k + 1 + s <= 7)
                 def _():
                     o = k + 1 + s
-                    left(o, i, 2 * s + i).wait_recv()
+                    left(o, i, NB * s + i).wait_recv()
 
                     @pl.when(k > 0)
                     def _():
-                        left(o, i, 2 * s + 2 + i).start()
+                        left(o, i, NB * s + NB + i).start()
 
             @pl.when(k - 1 - s >= 0)
             def _():
@@ -239,39 +241,36 @@
         d = PR.at[pl.ds(2 * zh, 2)]
         copy(d, d, ps.at[q], pr.at[q], {"core": 1 - c}).wait_recv()
 
+    def quarter(i):
+        return pl.ds(8 * i, 8)
+
     def c_copy(way, d, i, dev):
-        return copy(SB.at[d, half(i)], RB.at[way, d, half(i)], cs.at[d, i], cr.at[way, d, i], dev)
+        return copy(SB.at[d, quarter(i)], RB.at[way, d, quarter(i)], cs.at[d, i], cr.at[way, d, i], dev)
+
+    def c_send(way, pos, d, to):
+        for i in range(4):
+            mine = PF[d, c, quarter(i)] + PR[d, quarter(i)].astype(F32)
+
+            @pl.when(pos == 0)
+            def _():
+                SB[d, quarter(i)] = mine.astype(BF16)
+
+            @pl.when(pos > 0)
+            def _():
+                c_copy(way, d, i, {"zl": to}).wait_recv()
+                SB[d, quarter(i)] = (mine + RB[way, d, quarter(i)].astype(F32)).astype(BF16)
+
+            c_copy(way, d, i, {"zl": to}).start()
 
     def c_steps(lo, hi):
-        def one(way, pos, d, i, to):
-            mine = PF[d, c, half(i)] + PR[d, half(i)].astype(F32)
-
-            @pl.when(pos == 0)
-            def _():
-                SB[d, half(i)] = mine.astype(BF16)
-
-            @pl.when(pos > 0)
-            def _():
-                c_copy(way, d, i, {"zl": to}).wait_recv()
-                SB[d, half(i)] = (mine + RB[way, d, half(i)].astype(F32)).astype(BF16)
-
-            c_copy(way, d, i, {"zl": to}).start()
-
         def step(t, carry):
-            for i in range(2):
-                q = t - k - i
-                j = q // 2
-
-                @pl.when((q >= 0) & (lax.rem(q + 16, 2) == 0) & (7 - j > k))
-                def _():
-                    one(0, k, 7 - j, i, k + 1)
-
-                r = t - (7 - k) - i
-                m = r // 2
-
-                @pl.when((r >= 0) & (lax.rem(r + 16, 2) == 0) & (m < k))
-                def _():
-                    one(1, 7 - k, m, i, k - 1)
+            @pl.when((t >= k) & (k < 7))
+            def _():
+                c_send(0, k, 7 + k - t, k + 1)
+
+            @pl.when((t >= 7 - k) & (k > 0))
+            def _():
+                c_send(1, 7 - k, t - 7 + k, k - 1)
 
             return carry
 
@@ -282,13 +281,13 @@
 
         @pl.when(k > 0)
         def _():
-            for i in range(2):
+            for i in range(4):
                 c_copy(0, k, i, {"zl": k - 1}).wait_recv()
             HG[...] += RB[0, k].astype(F32)
 
         @pl.when(k < 7)
         def _():
-            for i in range(2):
+            for i in range(4):
                 c_copy(1, k, i, {"zl": k + 1}).wait_recv()
             HG[...] += RB[1, k].astype(F32)
 
@@ -296,7 +295,7 @@
         ug_ref[...] = (hg * act[...]).astype(BF16)
         gg_ref[...] = (hg * fac[...]).astype(BF16)
 
-    def dw(q, first=False):
+    def dw(q, first=False, last=False):
         zh = lax.rem(zo + q, 4)
         lhs = jnp.concatenate([HT[4 * zh + i] for i in range(4)], axis=1)
 
@@ -304,13 +303,17 @@
             cols = pl.ds(pl.multiple_of(n * 256, 256), 256)
             rhs = G[zh, :, :, :, cols].reshape(512, 256)
             res = jnp.dot(lhs, rhs, preferred_element_type=F32)
-            ACC[:, cols] = res if first else ACC[:, cols] + res
+            if last:
+                dw_ref[:, cols] = (ACC[:, cols] + res).astype(BF16)
+            else:
+                ACC[:, cols] = res if first else ACC[:, cols] + res
             return carry
 
         lax.fori_loop(0, 4, step, 0)
 
     z_first()
     y_first(0)
+    hidden()
     h_first()
     h_last()
     b_first()
@@ -319,63 +322,69 @@
     x_first(0)
     loads[3].wait()
     terms(0)
-    b_steps(0, 2)
+    b_steps(0,2)
     z_relay()
+    z_second()
     y_first(1)
     y_first(3)
-    b_steps(2, 3)
     y_relay(1)
     y_relay(3)
-    x_relay(0)
     y_last(1)
     y_last(3)
     x_first(1)
     x_first(3)
+    x_relay(0)
+    z_wait(0,2)
+    z_wait(1,2)
+    y_first(2)
     terms(1)
     terms(3)
-    b_steps(3, 4)
-    z_wait(0, 2)
-    z_wait(1, 2)
-    y_first(2)
-    b_steps(4, 5)
     y_relay(2)
     y_last(2)
     x_first(2)
     terms(2)
-    b_steps(5, 7)
-    for q in range(4):
-        terms_last(q)
+    terms_last(0)
+    terms_last(1)
+    terms_last(3)
+    terms_last(2)
+    c_steps(0,1)
+    b_steps(2,3)
+    c_steps(1,2)
     x_relay(1)
+    b_steps(3,4)
+    c_steps(2,3)
     x_relay(3)
-    c_steps(0, 4)
+    b_steps(4,5)
+    c_steps(3,4)
+    b_steps(5,6)
+    c_steps(4,5)
+    x_relay(2)
+    b_steps(6,7)
+    c_steps(5,6)
+    c_steps(6,7)
+    c_last()
     b_last()
     x_last(0)
-    dw(0, True)
-    c_steps(4, 7)
-    x_relay(2)
+    dw(0,first=True)
     x_last(1)
     dw(1)
-    c_steps(7, 10)
     x_last(3)
     dw(3)
-    c_steps(10, 14)
     x_last(2)
-    dw(2)
-    dw_ref[...] = ACC[...].astype(BF16)
-    c_last()
+    dw(2,last=True)
 
     for cp in sends:
         cp.wait_send()
 
     def drain_b(s, carry):
-        for i in range(2):
+        for i in range(NB):
             @pl.when((k - s >= 0) & (k < 7))
             def _():
-                right(k - s, i, 2 * s + i).wait_send()
+                right(k - s, i, NB * s + i).wait_send()
 
             @pl.when((k + s <= 7) & (k > 0))
             def _():
-                left(k + s, i, 2 * s + i).wait_send()
+                left(k + s, i, NB * s + i).wait_send()
 
         across(s).wait_send()
         return carry
@@ -385,7 +394,7 @@
     def drain_c(d, carry):
         @pl.when(d != k)
         def _():
-            for i in range(2):
+            for i in range(4):
                 c_copy(0, d, i, {"core": 1 - c}).wait_send()
 
         return carry
@@ -395,7 +404,7 @@
 
 def on_device(gate_pre, up_pre, out_grad, down_weight):
     dma = pltpu.SemaphoreType.DMA
-    any_spec = pl.BlockSpec(memory_space=pl.ANY)
+    hbm = pl.BlockSpec(memory_space=pltpu.MemorySpace.HBM)
     vmem = pl.BlockSpec(memory_space=pltpu.VMEM)
     act_shape = (32, 1664)
     return pl.pallas_call(
@@ -405,7 +414,7 @@
             jax.ShapeDtypeStruct(act_shape, BF16),
             jax.ShapeDtypeStruct(act_shape, BF16),
         ),
-        in_specs=[any_spec] * 4,
+        in_specs=[hbm] * 4,
         out_specs=(vmem,) * 3,
         scratch_shapes=[
             pltpu.VMEM((4, 4, 4, 32, 1024), BF16),
@@ -429,14 +438,14 @@
             dma((4, 4)), dma((4, 4)),
             dma((4, 4)), dma((4, 4)),
             dma((3,)), dma((3,)),
-            dma((16,)), dma((16,)),
-            dma((16,)), dma((16,)),
+            dma((8 * NB,)), dma((8 * NB,)),
+            dma((8 * NB,)), dma((8 * NB,)),
             dma((8,)), dma((8,)),
             dma((4,)), dma((4,)),
-            dma((8, 2)), dma((2, 8, 2)),
+            dma((8, 4)), dma((2, 8, 4)),
         ],
         compiler_params=pltpu.CompilerParams(
-            collective_id=0, has_side_effects=True, vmem_limit_bytes=48 * 1024 * 1024
+            collective_id=0, has_side_effects=True, vmem_limit_bytes=67043328
         ),
     )(gate_pre, up_pre, out_grad, down_weight)
 

time: 113 us -> 103 us (0.912)
  the two profiles are of different devices: /device:TPU:66 before, /device:TPU:36 now
where the time goes in v2:
time: 103 us
  Pallas kernels  96.8 us (94%)
  local copies, waits for them, and re-layouts  5.2 us (5%)
    pallas_call x1, Pallas kernels, on_device(): pl.pallas_call(kernel, out_shape=(jax.ShapeDtypeStruct((416, 1024), BF16)...  96.8 us
    unnamed x3, local copies, waits for them, and re-layouts  5.2 us

profile of v2, /device:TPU:36, one launch (start us, length us, event | category | flops | bytes accessed | tf_op | source)
XLA Modules:
  0.0 102.7 jit_solution(10224479827454350679)
XLA Ops:
  0.6 96.8 %shard_map.67 = (bf16[416,1024]{1,0:T(8,128)(2,1)}, bf16[32,1664]{1,0:T(8,128)(2,1)}, bf16[32,1664]{1,0:T(8,128)(2,1)}) custom-call(bf16[32,1664]{1,0:T(8,128)(2,1)} %gate_ref.1, bf16[32,1664]{1,0:T(8,128)(2,1)} %up_ref.1, bf16[32,1024]{1,0:T(8,128)(2,1)} %og_ref.1, bf16[1664,1024]{1,0:T(8,128)(2,1)} %w_ref.1), custom_call_target="tpu_custom_call" | custom-call | tf_op jit(solution)/shard_map/pallas_call | solution.py:410
  97.5 2.1 %copy.10 = bf16[416,1024]{1,0:T(8,128)(2,1)} copy(bf16[416,1024]{1,0:T(8,128)(2,1)} %get-tuple-element.6) | data formatting | bytes 1703936
  99.6 1.5 %copy.11 = bf16[32,1664]{1,0:T(8,128)(2,1)} copy(bf16[32,1664]{1,0:T(8,128)(2,1)} %get-tuple-element.7) | data formatting | bytes 212992
  101.1 1.5 %copy.12 = bf16[32,1664]{1,0:T(8,128)(2,1)} copy(bf16[32,1664]{1,0:T(8,128)(2,1)} %get-tuple-element.8) | data formatting | bytes 212992

commit v3 on v2

--- a/solution.py
+++ b/solution.py
@@ -19,8 +19,8 @@
 
 def kernel(
     gate_ref, up_ref, og_ref, w_ref,
-    dw_ref, gg_ref, ug_ref,
-    G, W, gv, uv, act, fac, HS, HX, HT, PF, PB, PR, RB, SB, HG, ACC,
+    dw_ref, hg_ref,
+    G, W, gv, uv, HS, HX, HT, PF, PB, PR, RB, SB, ACC,
     lsem, zs, zr, ys, yr, xs, xr, hs, hr, brs, brr, bls, blr, bps, bpr, ps, pr, cs, cr,
 ):
     zo, y, k, c, x = (lax.axis_index(a) for a in ("zh", "y", "zl", "core", "x"))
@@ -131,10 +131,7 @@
         g = gv[...].astype(F32)
         u = uv[...].astype(F32)
         sig = jax.nn.sigmoid(g)
-        a = g * sig
-        act[...] = a
-        fac[...] = u * sig * (1.0 + g * (1.0 - sig))
-        h = a * u
+        h = g * sig * u
         for s in range(4):
             rolled = h if s == 0 else pltpu.roll(h, 1664 - 416 * s, 1)
             HS[s] = rolled[:, :512].astype(BF16)
@@ -218,15 +215,16 @@
 
         lax.fori_loop(0, 8, step, 0)
 
-    def terms(q):
-        zh = lax.rem(zo + q, 4)
-        rows = G[zh, :, x].reshape(128, 1024)
+    def terms(*groups):
+        zhs = [lax.rem(zo + q, 4) for q in groups]
+        rows = jnp.concatenate([G[zh, :, x].reshape(128, 1024) for zh in zhs], axis=0)
 
         def part(n0, nn):
             res = lax.dot_general(rows, W[pl.ds(n0, nn), :], NT, preferred_element_type=F32)
-            res = res.reshape(2, 2, 32, nn)
-            PF[pl.ds(2 * zh, 2), :, :, pl.ds(n0, nn)] = res
-            PB[pl.ds(2 * zh, 2), :, :, pl.ds(n0, nn)] = res.astype(BF16)
+            for n, zh in enumerate(zhs):
+                one = res[128 * n : 128 * n + 128].reshape(2, 2, 32, nn)
+                PF[pl.ds(2 * zh, 2), :, :, pl.ds(n0, nn)] = one
+                PB[pl.ds(2 * zh, 2), :, :, pl.ds(n0, nn)] = one.astype(BF16)
 
         def step(i, carry):
             part(pl.multiple_of(i * 256, 256), 256)
@@ -234,7 +232,9 @@
 
         lax.fori_loop(0, 6, step, 0)
         part(1536, 128)
-        send(PB.at[pl.ds(2 * zh, 2), 1 - c], PR.at[pl.ds(2 * zh, 2)], ps.at[q], pr.at[q], {"core": 1 - c})
+        for q, zh in zip(groups, zhs):
+            pair = PB.at[pl.ds(2 * zh, 2), 1 - c]
+            send(pair, PR.at[pl.ds(2 * zh, 2)], ps.at[q], pr.at[q], {"core": 1 - c})
 
     def terms_last(q):
         zh = lax.rem(zo + q, 4)
@@ -277,23 +277,20 @@
         lax.fori_loop(lo, hi, step, 0)
 
     def c_last():
-        HG[...] = PF[k, c] + PR[k].astype(F32)
+        hg_ref[...] = PF[k, c] + PR[k].astype(F32)
 
         @pl.when(k > 0)
         def _():
             for i in range(4):
                 c_copy(0, k, i, {"zl": k - 1}).wait_recv()
-            HG[...] += RB[0, k].astype(F32)
+            hg_ref[...] += RB[0, k].astype(F32)
 
         @pl.when(k < 7)
         def _():
             for i in range(4):
                 c_copy(1, k, i, {"zl": k + 1}).wait_recv()
-            HG[...] += RB[1, k].astype(F32)
-
-        hg = HG[...]
-        ug_ref[...] = (hg * act[...]).astype(BF16)
-        gg_ref[...] = (hg * fac[...]).astype(BF16)
+            hg_ref[...] += RB[1, k].astype(F32)
+
 
     def dw(q, first=False, last=False):
         zh = lax.rem(zo + q, 4)
@@ -320,29 +317,29 @@
     y_relay(0)
     y_last(0)
     x_first(0)
+    b_steps(0,1)
+    z_relay()
     loads[3].wait()
     terms(0)
-    b_steps(0,2)
-    z_relay()
+    b_steps(1,2)
     z_second()
     y_first(1)
     y_first(3)
     y_relay(1)
     y_relay(3)
+    z_wait(0,2)
+    z_wait(1,2)
+    y_first(2)
     y_last(1)
     y_last(3)
     x_first(1)
     x_first(3)
-    x_relay(0)
-    z_wait(0,2)
-    z_wait(1,2)
-    y_first(2)
-    terms(1)
-    terms(3)
+    terms(1,3)
     y_relay(2)
     y_last(2)
     x_first(2)
     terms(2)
+    x_relay(0)
     terms_last(0)
     terms_last(1)
     terms_last(3)
@@ -361,13 +358,13 @@
     x_relay(2)
     b_steps(6,7)
     c_steps(5,6)
-    c_steps(6,7)
-    c_last()
     b_last()
     x_last(0)
     dw(0,first=True)
+    c_steps(6,7)
     x_last(1)
     dw(1)
+    c_last()
     x_last(3)
     dw(3)
     x_last(2)
@@ -407,22 +404,19 @@
     hbm = pl.BlockSpec(memory_space=pltpu.MemorySpace.HBM)
     vmem = pl.BlockSpec(memory_space=pltpu.VMEM)
     act_shape = (32, 1664)
-    return pl.pallas_call(
+    weight_grad, hidden_grad = pl.pallas_call(
         kernel,
         out_shape=(
             jax.ShapeDtypeStruct((416, 1024), BF16),
-            jax.ShapeDtypeStruct(act_shape, BF16),
-            jax.ShapeDtypeStruct(act_shape, BF16),
+            jax.ShapeDtypeStruct(act_shape, F32),
         ),
         in_specs=[hbm] * 4,
-        out_specs=(vmem,) * 3,
+        out_specs=(vmem,) * 2,
         scratch_shapes=[
             pltpu.VMEM((4, 4, 4, 32, 1024), BF16),
             pltpu.VMEM((1664, 1024), BF16),
             pltpu.VMEM(act_shape, BF16),
             pltpu.VMEM(act_shape, BF16),
-            pltpu.VMEM(act_shape, F32),
-            pltpu.VMEM(act_shape, F32),
             pltpu.VMEM((4, 32, 512), BF16),
             pltpu.VMEM((4, 32, 512), BF16),
             pltpu.VMEM((16, 416, 128), BF16),
@@ -431,7 +425,6 @@
             pltpu.VMEM((8, 32, 1664), BF16),
             pltpu.VMEM((2, 8, 32, 1664), BF16),
             pltpu.VMEM((8, 32, 1664), BF16),
-            pltpu.VMEM(act_shape, F32),
             pltpu.VMEM((416, 1024), F32),
             dma((4,)),
             dma((2, 3)), dma((2, 3)),
@@ -448,6 +441,12 @@
             collective_id=0, has_side_effects=True, vmem_limit_bytes=67043328
         ),
     )(gate_pre, up_pre, out_grad, down_weight)
+    gate_vals = gate_pre.astype(F32)
+    sigma = jax.nn.sigmoid(gate_vals)
+    up_grad = (hidden_grad * (gate_vals * sigma)).astype(BF16)
+    slope = up_pre.astype(F32) * sigma * (1.0 + gate_vals * (1.0 - sigma))
+    gate_grad = (hidden_grad * slope).astype(BF16)
+    return weight_grad, gate_grad, up_grad
 
 
 def solution(mesh):

time: 103 us -> 97.4 us (0.946)
  the two profiles are of different devices: /device:TPU:36 before, /device:TPU:12 now
where the time goes in v3:
time: 97.4 us; the launch traced here: 97.2 us
  Pallas kernels  92.6 us (95%)
  local copies, waits for them, and re-layouts  2.11 us (2%)
  other arithmetic  1.84 us (2%)
    pallas_call x1, Pallas kernels, on_device(): pl.pallas_call(kernel, out_shape=(jax.ShapeDtypeStruct((416, 1024), BF16)...  92.6 us
    unnamed x1, local copies, waits for them, and re-layouts  2.11 us

profile of v3, /device:TPU:12, one launch (start us, length us, event | category | flops | bytes accessed | tf_op | source)
XLA Modules:
  0.0 97.2 jit_solution(6251805547622114689)
XLA Ops:
  0.6 92.6 %shard_map.67 = (bf16[416,1024]{1,0:T(8,128)(2,1)}, f32[32,1664]{1,0:T(8,128)}) custom-call(bf16[32,1664]{1,0:T(8,128)(2,1)} %gate_ref.1, bf16[32,1664]{1,0:T(8,128)(2,1)} %up_ref.1, bf16[32,1024]{1,0:T(8,128)(2,1)} %og_ref.1, bf16[1664,1024]{1,0:T(8,128)(2,1)} %w_ref.1), custom_call_target="tpu_custom_call" | custom-call | tf_op jit(solution)/shard_map/pallas_call | solution.py:407
  93.2 1.8 %fusion.8 = (bf16[32,1664]{1,0:T(8,128)(2,1)}, bf16[32,1664]{1,0:T(8,128)(2,1)}) fusion(f32[32,1664]{1,0:T(8,128)} %get-tuple-element.6, bf16[32,1664]{1,0:T(8,128)(2,1)} %gate_ref.1, bf16[32,1664]{1,0:T(8,128)(2,1)} %up_ref.1), kind=kLoop, calls=%fused_computation.11 | loop fusion | flops 798720 | bytes 638976 | tf_op jit(solution)/shard_map/convert_element_type | solution.py:446
  95.1 2.1 %copy.8 = bf16[416,1024]{1,0:T(8,128)(2,1)} copy(bf16[416,1024]{1,0:T(8,128)(2,1)} %get-tuple-element.12) | data formatting | bytes 1703936

commit v4 on v3

--- a/solution.py
+++ b/solution.py
@@ -325,6 +325,7 @@
     z_second()
     y_first(1)
     y_first(3)
+    b_steps(2,3)
     y_relay(1)
     y_relay(3)
     z_wait(0,2)
@@ -345,7 +346,6 @@
     terms_last(3)
     terms_last(2)
     c_steps(0,1)
-    b_steps(2,3)
     c_steps(1,2)
     x_relay(1)
     b_steps(3,4)
@@ -364,9 +364,9 @@
     c_steps(6,7)
     x_last(1)
     dw(1)
-    c_last()
     x_last(3)
     dw(3)
+    c_last()
     x_last(2)
     dw(2,last=True)
 

time: 97.4 us -> 95.6 us (0.982)
  the two profiles are of different devices: /device:TPU:12 before, /device:TPU:32 now
where the time goes in v4:
time: 95.6 us; the launch traced here: 95.4 us
  Pallas kernels  90.8 us (95%)
  local copies, waits for them, and re-layouts  2.11 us (2%)
  other arithmetic  1.84 us (2%)
    pallas_call x1, Pallas kernels, on_device(): pl.pallas_call(kernel, out_shape=(jax.ShapeDtypeStruct((416, 1024), BF16)...  90.8 us
    unnamed x1, local copies, waits for them, and re-layouts  2.11 us

profile of v4, /device:TPU:32, one launch (start us, length us, event | category | flops | bytes accessed | tf_op | source)
XLA Modules:
  0.0 95.4 jit_solution(3338468711697302608)
XLA Ops:
  0.6 90.8 %shard_map.67 = (bf16[416,1024]{1,0:T(8,128)(2,1)}, f32[32,1664]{1,0:T(8,128)}) custom-call(bf16[32,1664]{1,0:T(8,128)(2,1)} %gate_ref.1, bf16[32,1664]{1,0:T(8,128)(2,1)} %up_ref.1, bf16[32,1024]{1,0:T(8,128)(2,1)} %og_ref.1, bf16[1664,1024]{1,0:T(8,128)(2,1)} %w_ref.1), custom_call_target="tpu_custom_call" | custom-call | tf_op jit(solution)/shard_map/pallas_call | solution.py:407
  91.4 1.8 %fusion.8 = (bf16[32,1664]{1,0:T(8,128)(2,1)}, bf16[32,1664]{1,0:T(8,128)(2,1)}) fusion(f32[32,1664]{1,0:T(8,128)} %get-tuple-element.6, bf16[32,1664]{1,0:T(8,128)(2,1)} %gate_ref.1, bf16[32,1664]{1,0:T(8,128)(2,1)} %up_ref.1), kind=kLoop, calls=%fused_computation.11 | loop fusion | flops 798720 | bytes 638976 | tf_op jit(solution)/shard_map/convert_element_type | solution.py:446
  93.3 2.1 %copy.8 = bf16[416,1024]{1,0:T(8,128)(2,1)} copy(bf16[416,1024]{1,0:T(8,128)(2,1)} %get-tuple-element.12) | data formatting | bytes 1703936
